TPU v7x, 128 devices: a whole 4x4x4 slice. The times are simulated.
128 devices in a mesh: patch: 16 (over z, y), body: 8 (over x, core).
Axes of the slice: x: 4, y: 4, z: 4, core: 2. Of those that a mesh axis runs over, the one named last changes fastest.
Arguments:
- donors: bfloat16 [120, 262144], P(None, ('patch', 'body')), may hold values from -3 to 3
- owner: int32 [262144, 1], P(('patch', 'body')), may hold values from 0 to 127; in each aligned block of 2048 rows (0 to 2047, 2048 to 4095, ...) at most 32 rows name the same one
- slot: int32 [262144], P(('patch', 'body')), may hold values from 0 to 255
- target: float32 [32, 1024, 3], P('patch', 'body'), may hold values from -6 to 6
- weight_a: bfloat16 [3, 5, 96], replicated, may hold values from -1.5 to 1.5
- weight_b: bfloat16 [9, 96, 96], replicated, may hold values from -0.21875 to 0.21875
- weight_h: bfloat16 [2304, 3], replicated, may hold values from -0.125 to 0.125
Outputs:
- stress: float32 [32, 1024, 3], P('patch', 'body')
- profile_grad: float32 [120, 32, 1024], P(None, 'patch', 'body')
- grad_a: float32 [3, 5, 96], replicated
- grad_b: float32 [9, 96, 96], replicated
- grad_h: float32 [2304, 3], replicated
Inputs may be any that keep to these rules, and one draw needn't show every extreme that they name: Of the donor rows of one device, at most 32 name the same owner; some owner gets exactly 32 from some device.
All inputs are finite; a program needn't handle non-finite values.
Results may differ from a plain program's by a relative error of at most 0.006.
Values may be sent and summed in bfloat16 or wider, within the bound.
No kernel may reach another device: no remote copies, remote signals or barrier semaphores. Data moves between devices by JAX's collectives and lax.ppermute only.
A program may use at most 128 MiB of HBM per device.

v0:
```python
import jax
import jax.numpy as jnp
from jax import lax
from jax.sharding import PartitionSpec as P


def with_halo(cells, sides, width):
    for axis, dim in sides:
        count = lax.axis_size(axis)
        ends = count - 1
        head = lax.slice_in_dim(cells, 0, width, axis=dim)
        tail = lax.slice_in_dim(cells, cells.shape[dim] - width, cells.shape[dim], axis=dim)
        cells = jnp.concatenate(
            [
                lax.ppermute(tail, axis, [(i, (i + 1) % count) for i in range(ends)]),
                cells,
                lax.ppermute(head, axis, [((i + 1) % count, i) for i in range(ends)]),
            ],
            axis=dim,
        )
    return cells


def silu_slope(value):
    sig = jax.nn.sigmoid(value)
    return sig * (1.0 + value * (1.0 - sig))


def layer_one(prof, weight_a, heights, fields, chans):
    size_x, size_y = (prof.shape[0], prof.shape[1])
    prof_four = prof.reshape(size_x, size_y, heights, fields)
    padded_h = jnp.pad(prof_four, ((0, 0), (0, 0), (2, 2), (0, 0)))
    unfold = jnp.concatenate(
        [padded_h[:, :, 2 * tap : 2 * tap + heights] for tap in range(3)], axis=3
    ).reshape(size_x * size_y * heights, 3 * fields)
    pre_a = jnp.dot(unfold, weight_a.reshape(3 * fields, chans), preferred_element_type=jnp.float32)
    act_one = jax.nn.silu(pre_a).astype(jnp.bfloat16)
    return (unfold, pre_a, act_one)


def conv_tangent(padded, weight_b, size_x, size_y):
    chans = padded.shape[3]
    pre_b = jnp.zeros((size_x * size_y * padded.shape[2], chans), jnp.float32)
    for tap in range(9):
        shift_x, shift_y = (tap // 3, tap % 3)
        piece = padded[shift_x : shift_x + size_x, shift_y : shift_y + size_y].reshape(-1, chans)
        pre_b = pre_b + jnp.dot(piece, weight_b[tap], preferred_element_type=jnp.float32)
    return pre_b


def shards(donors, owner, slot, target, weight_a, weight_b, weight_h):
    tile_x, tile_y = (target.shape[0], target.shape[1])
    fields, chans = (weight_a.shape[1], weight_a.shape[2])
    heights = weight_h.shape[0] // chans
    width = heights * fields
    n_patch = lax.axis_size("patch")
    n_body = lax.axis_size("body")
    n_dev = n_patch * n_body
    rows = donors.shape[1]
    cap = 2 * rows // n_dev
    dest = owner[:, 0]
    hits = (dest[:, None] == jnp.arange(n_dev, dtype=jnp.int32)[None, :]).astype(jnp.int32)
    before = jnp.cumsum(hits, axis=0) - hits
    rank = jnp.sum(before * hits, axis=1)
    place = dest * cap + rank
    outbox = jnp.zeros((width, n_dev * cap), jnp.bfloat16).at[:, place].set(donors)
    outslot = jnp.zeros((n_dev * cap,), jnp.int32).at[place].set(slot)
    inbox, inslot = (
        lax.all_to_all(
            outbox.reshape(width, n_dev, cap),
            ("patch", "body"),
            split_axis=1,
            concat_axis=1,
            tiled=True,
        ),
        lax.all_to_all(
            outslot.reshape(1, n_dev, cap),
            ("patch", "body"),
            split_axis=1,
            concat_axis=1,
            tiled=True,
        ),
    )
    points = tile_x * tile_y
    cells = points * heights
    summed = (
        jnp.zeros((points, width), jnp.float32)
        .at[inslot.reshape(-1)]
        .add(jnp.transpose(inbox.reshape(width, -1)).astype(jnp.float32))
    )
    profile = summed.astype(jnp.bfloat16).reshape(tile_x, tile_y, width)
    contract_rows = (((0,), (0,)), ((), ()))
    contract_cols = (((1,), (1,)), ((), ()))
    unfold, pre_a, act_one = layer_one(profile, weight_a, heights, fields, chans)
    padded = with_halo(
        act_one.reshape(tile_x, tile_y, heights, chans), (("patch", 0), ("body", 1)), 1
    )
    pre_b = conv_tangent(padded, weight_b, tile_x, tile_y)
    act_two = (act_one.astype(jnp.float32) + jax.nn.silu(pre_b)).astype(jnp.bfloat16)
    features = act_two.reshape(points, heights * chans)
    stress = jnp.dot(features, weight_h, preferred_element_type=jnp.float32)
    err = (stress - target.reshape(points, 3)).astype(jnp.bfloat16)
    grad_h = lax.dot_general(features, err, contract_rows, preferred_element_type=jnp.float32)
    dz_two = lax.dot_general(
        err, weight_h, contract_cols, preferred_element_type=jnp.float32
    ).reshape(cells, chans)
    da_two = (dz_two * silu_slope(pre_b)).astype(jnp.bfloat16)
    parts_b = []
    for tap in range(9):
        shift_x, shift_y = (tap // 3, tap % 3)
        piece = padded[shift_x : shift_x + tile_x, shift_y : shift_y + tile_y].reshape(cells, chans)
        parts_b.append(
            lax.dot_general(piece, da_two, contract_rows, preferred_element_type=jnp.float32)
        )
    grad_b = jnp.stack(parts_b)
    da_pad = with_halo(
        da_two.reshape(tile_x, tile_y, heights, chans), (("patch", 0), ("body", 1)), 1
    )
    dz_one = dz_two
    for tap in range(9):
        shift_x, shift_y = (tap // 3, tap % 3)
        back = da_pad[
            2 - shift_x : 2 - shift_x + tile_x, 2 - shift_y : 2 - shift_y + tile_y
        ].reshape(cells, chans)
        dz_one = dz_one + lax.dot_general(
            back, weight_b[tap], contract_cols, preferred_element_type=jnp.float32
        )
    da_one = (dz_one * silu_slope(pre_a)).astype(jnp.bfloat16)
    grad_a = lax.dot_general(
        unfold, da_one, contract_rows, preferred_element_type=jnp.float32
    ).reshape(3, fields, chans)
    da_heights = jnp.pad(
        da_one.reshape(tile_x, tile_y, heights, chans), ((0, 0), (0, 0), (2, 2), (0, 0))
    )
    profile_grad = jnp.zeros((cells, fields), jnp.float32)
    for tap in range(3):
        moved = da_heights[:, :, 4 - 2 * tap : 4 - 2 * tap + heights].reshape(cells, chans)
        profile_grad = profile_grad + lax.dot_general(
            moved, weight_a[tap], contract_cols, preferred_element_type=jnp.float32
        )
    grad_a, grad_b, grad_h = lax.psum((grad_a, grad_b, grad_h), ("patch", "body"))
    scale = 1.0 / jnp.sqrt(jnp.float32(points * n_dev))
    grad_out = jnp.transpose(profile_grad.reshape(tile_x, tile_y, width), (2, 0, 1))
    return (
        stress.reshape(tile_x, tile_y, 3),
        grad_out,
        grad_a * scale,
        grad_b * scale,
        grad_h * scale,
    )


def solution(mesh):
    placed = (
        P(None, ("patch", "body")),
        P(("patch", "body"), None),
        P(("patch", "body")),
        P("patch", "body", None),
        P(),
        P(),
        P(),
    )
    return jax.shard_map(
        shards,
        mesh=mesh,
        in_specs=placed,
        out_specs=(P("patch", "body", None), P(None, "patch", "body"), P(), P(), P()),
        check_vma=False,
    )
```

profile of v0, /device:TPU:1, one launch (start us, length us, event | category | flops | bytes accessed | tf_op | source)
XLA Modules:
  0.0 441.9 jit_solution(4679156785782722529)
XLA Ops:
  9.8 8.2 %scatter_custom_fusion = s32[4096]{0:T(1024)S(1)} fusion(s32[2048]{0:T(1024)S(1)} %bitcast.259, s32[2048]{0:T(1024)} %param.9, s32[]{:T(128)} %constant.9.clone.1), kind=kCustom, calls=%fused_computation.126 | custom fusion | bytes 16896 | tf_op jit(solution)/shard_map/scatter | solution.py:67
  18.8 11.5 %all-to-all-start = ((s32[1,128,32]{2,0,1:T(1,128)}), s32[1,128,32]{2,0,1:T(1,128)S(1)}, u32[]{:S(2)}, u32[]{:S(2)}) async-start(s32[1,128,32]{2,0,1:T(1,128)} %bitcast.7), calls=%async_computation | async-start | bytes 131072 | tf_op jit(solution)/shard_map/all_to_all | solution.py:76
  30.6 6.8 %scatter_custom_fusion.1 = bf16[120,4096]{0,1:T(8,128)(2,1)} fusion(s32[2048]{0:T(1024)S(1)} %bitcast.260, bf16[2048,120]{1,0:T(8,128)(2,1)S(1)} %copy.51, bf16[]{:T(256)} %constant.6.clone.1), kind=kCustom, calls=%fused_computation.68 | custom fusion | bytes 983042 | tf_op jit(solution)/shard_map/scatter | solution.py:66
  37.4 2.4 all-to-all-done
  39.8 7.4 %all-to-all-start.1 = ((bf16[120,128,32]{0,2,1:T(8,128)(2,1)}), bf16[120,128,32]{0,2,1:T(8,128)(2,1)S(1)}, u32[]{:S(2)}, u32[]{:S(2)}) async-start(bf16[120,128,32]{0,2,1:T(8,128)(2,1)} %bitcast.10), calls=%async_computation.1 | async-start | bytes 2097152 | tf_op jit(solution)/shard_map/all_to_all | solution.py:69
  48.7 17.7 %all-to-all-done.1 = bf16[120,128,32]{0,2,1:T(8,128)(2,1)S(1)} async-done(((bf16[120,128,32]{0,2,1:T(8,128)(2,1)}), bf16[120,128,32]{0,2,1:T(8,128)(2,1)S(1)}, u32[]{:S(2)}, u32[]{:S(2)}) %all-to-all-start.1) | async-done | bytes 983072 | tf_op jit(solution)/shard_map/all_to_all | solution.py:69
  66.4 24.0 %scatter_custom_fusion.2 = f32[256,120]{1,0:T(8,128)S(1)} fusion(s32[4096]{0:T(1024)S(1)} %bitcast.258, bf16[120,4096]{0,1:T(8,128)(2,1)S(1)} %bitcast.247, f32[]{:T(128)} %constant.8.clone.1), kind=kCustom, calls=%fused_computation.36 | custom fusion | flops 983040 | bytes 1171460 | tf_op jit(solution)/shard_map/scatter-add | solution.py:89
  90.5 1.1 concatenate.51
  93.9 2.2 multiply_convert_fusion.1
  98.1 2.2 copy.60
  100.3 2.3 copy.61
  102.7 1.3 collective-permute-start.1
  104.0 1.2 copy.57
  105.1 2.3 copy.58
  107.5 4.8 %collective-permute-start = (bf16[1,128,24,96]{1,3,2,0:T(8,128)(2,1)}, bf16[1,128,24,96]{1,3,2,0:T(8,128)(2,1)}, u32[]{:S(2)}, u32[]{:S(2)}) collective-permute-start(bf16[1,128,24,96]{1,3,2,0:T(8,128)(2,1)} %copy.58), channel_id=1, source_target_pairs={{0,8},{8,16},{16,24},{24,32},{32,40},{40,48},{48,56},{56,64},{64,7... | collective-permute-start | bytes 1769480 | tf_op jit(solution)/shard_map/ppermute | solution.py:15
  114.2 5.0 %collective-permute-done.1 = bf16[1,128,24,96]{1,3,2,0:T(8,128)(2,1)} collective-permute-done((bf16[1,128,24,96]{1,3,2,0:T(8,128)(2,1)}, bf16[1,128,24,96]{1,3,2,0:T(8,128)(2,1)}, u32[]{:S(2)}, u32[]{:S(2)}) %collective-permute-start.1) | collective-permute-done | bytes 589856 | tf_op jit(solution)/shard_map/ppermute | solution.py:17
  119.2 2.3 copy.63
  121.5 2.1 collective-permute-done
  123.6 2.3 copy.62
  128.0 3.7 collective-permute-start.3
  131.7 2.8 collective-permute-start.2
  135.2 2.2 pad_maximum_fusion
  137.5 1.7 fusion.68
  144.7 2.5 add_convert_fusion
  148.2 1.3 reshape.183
  149.9 2.1 fusion.72
  151.9 4.7 %reshape.186 = f32[6144,96]{1,0:T(8,128)} reshape(f32[256,2304]{1,0:T(8,128)} %fusion.72) | data formatting | bytes 4718592 | tf_op jit(solution)/shard_map/reshape | solution.py:106
  156.6 2.6 copy.75
  159.2 3.4 multiply_convert_fusion
  174.9 1.3 copy.69
  176.3 5.0 %collective-permute-start.4 = (bf16[1,128,24,96]{1,3,2,0:T(8,128)(2,1)}, bf16[1,128,24,96]{1,3,2,0:T(8,128)(2,1)}, u32[]{:S(2)}, u32[]{:S(2)}) collective-permute-start(bf16[1,128,24,96]{1,3,2,0:T(8,128)(2,1)} %copy.69), channel_id=1, source_target_pairs={{0,8},{8,16},{16,24},{24,32},{32,40},{40,48},{48,56},{56,64},{64,7... | collective-permute-start | bytes 1769480 | tf_op jit(solution)/shard_map/ppermute | solution.py:15
  181.3 1.4 copy.71
  182.7 1.3 copy.72
  184.0 1.3 collective-permute-start.5
  185.3 1.2 fusion.5
  188.0 2.2 fusion.73
  190.2 145.0 %all-reduce.5.cloned.1.call-done = f32[9,96,96]{2,1,0:T(8,128)} async-done(((f32[9,96,96]{2,1,0:T(8,128)}), f32[9,96,96]{2,1,0:T(8,128)}) %all-reduce.5.cloned.1.call-update) | async-done | bytes 331792 | tf_op jit(solution)/shard_map/psum | solution.py:141
  335.2 1.8 broadcast_multiply_fusion
  337.1 1.5 copy.73
  338.5 2.3 copy.74
  341.7 3.5 collective-permute-start.7
  345.2 1.9 collective-permute-start.6
  347.8 2.6 collective-permute-done.6
  350.3 2.5 maximum_maximum_fusion.1
  361.2 1.1 fusion.1
  363.8 64.4 %all-reduce.2 = (f32[3,5,96]{2,1,0:T(8,128)S(1)}, f32[2304,3]{0,1:T(4,128)S(1)}) all-reduce(f32[3,5,96]{2,1,0:T(8,128)S(1)} %fusion.3, f32[2304,3]{0,1:T(4,128)S(1)} %copy-done.33), channel_id=1, replica_groups=mesh['patch'=16,'body'=8] {'patch','body'}, use_global_device_ids=true, to_apply=%region_6.7 | all-reduce | flops 8352 | bytes 66816 | tf_op jit(solution)/shard_map/psum | solution.py:141
  429.4 1.2 pad_slice_fusion
  431.9 1.1 copy.82
  (159 shorter events, 50.0 us)
Async XLA Ops:
  7.2 142.3 %copy-start = (bf16[2304,3]{0,1:T(4,128)(2,1)S(1)}, bf16[2304,3]{0,1:T(4,128)(2,1)}, u32[]{:S(2)}) copy-start(bf16[2304,3]{0,1:T(4,128)(2,1)} %param.13) | copy-start | bytes 41476
  8.5 21.8 %copy-start.30 = (bf16[120,2048]{1,0:T(8,128)(2,1)S(1)}, bf16[120,2048]{1,0:T(8,128)(2,1)}, u32[]{:S(2)}) copy-start(bf16[120,2048]{1,0:T(8,128)(2,1)} %param.7) | copy-start | bytes 1474564
  18.8 21.1 %all-to-all-start = ((s32[1,128,32]{2,0,1:T(1,128)}), s32[1,128,32]{2,0,1:T(1,128)S(1)}, u32[]{:S(2)}, u32[]{:S(2)}) async-start(s32[1,128,32]{2,0,1:T(1,128)} %bitcast.7), calls=%async_computation | async-start | bytes 131072 | tf_op jit(solution)/shard_map/all_to_all | solution.py:76
  30.6 16.7 %copy-start.36 = (bf16[3,5,96]{2,0,1:T(4,128)(2,1)S(1)}, bf16[3,5,96]{2,0,1:T(4,128)(2,1)}, u32[]{:S(2)}) copy-start(bf16[3,5,96]{2,0,1:T(4,128)(2,1)} %param.11) | copy-start | bytes 8644
  39.8 26.6 %all-to-all-start.1 = ((bf16[120,128,32]{0,2,1:T(8,128)(2,1)}), bf16[120,128,32]{0,2,1:T(8,128)(2,1)S(1)}, u32[]{:S(2)}, u32[]{:S(2)}) async-start(bf16[120,128,32]{0,2,1:T(8,128)(2,1)} %bitcast.10), calls=%async_computation.1 | async-start | bytes 2097152 | tf_op jit(solution)/shard_map/all_to_all | solution.py:69
  47.2 288.0 %all-reduce.5.cloned.1.call-start = ((), (), s32[]{:S(2)}) async-start(), calls=%async_computation.2 | async-start | bytes 884736 | tf_op jit(solution)/shard_map/psum | solution.py:141
  92.4 3.7 copy-start.31
  93.1 2.9 copy-start.32
  96.1 48.6 %copy-start.4 = (bf16[6144,96]{0,1:T(8,128)(2,1)}, bf16[6144,96]{0,1:T(8,128)(2,1)S(1)}, u32[]{:S(2)}) copy-start(bf16[6144,96]{0,1:T(8,128)(2,1)S(1)} %get-tuple-element.54) | copy-start | bytes 3538948
  102.7 16.5 %collective-permute-start.1 = (bf16[1,128,24,96]{1,3,2,0:T(8,128)(2,1)}, bf16[1,128,24,96]{1,3,2,0:T(8,128)(2,1)}, u32[]{:S(2)}, u32[]{:S(2)}) collective-permute-start(bf16[1,128,24,96]{1,3,2,0:T(8,128)(2,1)} %copy.61), channel_id=1, source_target_pairs={{8,0},{16,8},{24,16},{32,24},{40,32},{48,40},{56,48},{64,56},{72,6... | collective-permute-start | bytes 1769480 | tf_op jit(solution)/shard_map/ppermute | solution.py:17
  107.5 16.1 %collective-permute-start = (bf16[1,128,24,96]{1,3,2,0:T(8,128)(2,1)}, bf16[1,128,24,96]{1,3,2,0:T(8,128)(2,1)}, u32[]{:S(2)}, u32[]{:S(2)}) collective-permute-start(bf16[1,128,24,96]{1,3,2,0:T(8,128)(2,1)} %copy.58), channel_id=1, source_target_pairs={{0,8},{8,16},{16,24},{24,32},{32,40},{40,48},{48,56},{56,64},{64,7... | collective-permute-start | bytes 1769480 | tf_op jit(solution)/shard_map/ppermute | solution.py:15
  125.9 1.2 copy-start.20
  125.9 1.4 copy-start.21
  127.3 7.1 %copy-start.27 = (bf16[9,96,96]{2,1,0:T(8,128)(2,1)S(1)}, bf16[9,96,96]{2,1,0:T(8,128)(2,1)}, u32[]{:S(2)}) copy-start(bf16[9,96,96]{2,1,0:T(8,128)(2,1)} %param.12) | copy-start | bytes 497668
  128.0 7.2 %copy-start.18 = (bf16[2,128,24,96]{3,2,1,0:T(8,128)(2,1)}, bf16[2,128,24,96]{3,2,1,0:T(8,128)(2,1)S(1)}, u32[]{:S(2)}) copy-start(bf16[2,128,24,96]{3,2,1,0:T(8,128)(2,1)S(1)} %get-tuple-element.47) | copy-start | bytes 3538948
  128.0 16.0 %copy-start.16 = (bf16[2,128,24,96]{3,2,1,0:T(8,128)(2,1)}, bf16[2,128,24,96]{3,2,1,0:T(8,128)(2,1)S(1)}, u32[]{:S(2)}) copy-start(bf16[2,128,24,96]{3,2,1,0:T(8,128)(2,1)S(1)} %get-tuple-element.46) | copy-start | bytes 3538948
  128.0 7.2 %collective-permute-start.3 = (bf16[4,1,24,96]{3,2,1,0:T(8,128)(2,1)S(1)}, bf16[4,1,24,96]{3,2,1,0:T(8,128)(2,1)S(1)}, u32[]{:S(2)}, u32[]{:S(2)}) collective-permute-start(bf16[4,1,24,96]{3,2,1,0:T(8,128)(2,1)S(1)} %get-tuple-element.40), channel_id=1, source_target_pairs={{1,0},{2,1},{3,2},{4,3},{5,4},{6,5},{7,6},{9,8},{10,9},{11,10},{12... | collective-permute-start | bytes 55304 | tf_op jit(solution)/shard_map/ppermute | solution.py:17
  131.7 3.5 collective-permute-start.2
  139.1 1.1 copy-start.12
  139.2 1.8 copy-start.14
  139.2 2.1 copy-start.10
  139.2 3.4 copy-start.8
  139.2 4.1 copy-start.6
  139.2 5.5 %copy-start.24 = (bf16[2,128,24,96]{3,2,1,0:T(8,128)(2,1)}, bf16[2,128,24,96]{3,2,1,0:T(8,128)(2,1)S(1)}, u32[]{:S(2)}) copy-start(bf16[2,128,24,96]{3,2,1,0:T(8,128)(2,1)S(1)} %get-tuple-element.28) | copy-start | bytes 3538948
  148.2 1.3 copy-start.35
  149.5 2.5 copy-start.23
  159.2 3.4 copy-start.2
  159.2 3.4 copy-start.15
  163.2 1.6 copy-start.19
  164.8 1.4 copy-start.13
  166.2 1.4 copy-start.11
  167.6 1.3 copy-start.5
  168.9 1.4 copy-start.9
  170.3 1.4 copy-start.7
  171.7 1.4 copy-start.17
  173.8 0.8 copy-start.29
  176.2 9.1 %copy-start.25 = (bf16[2,128,24,96]{3,2,1,0:T(8,128)(2,1)S(1)}, bf16[2,128,24,96]{3,2,1,0:T(8,128)(2,1)}, u32[]{:S(2)}) copy-start(bf16[2,128,24,96]{3,2,1,0:T(8,128)(2,1)} %copy-done.24) | copy-start | bytes 3538948
  176.3 160.8 %collective-permute-start.4 = (bf16[1,128,24,96]{1,3,2,0:T(8,128)(2,1)}, bf16[1,128,24,96]{1,3,2,0:T(8,128)(2,1)}, u32[]{:S(2)}, u32[]{:S(2)}) collective-permute-start(bf16[1,128,24,96]{1,3,2,0:T(8,128)(2,1)} %copy.69), channel_id=1, source_target_pairs={{0,8},{8,16},{16,24},{24,32},{32,40},{40,48},{48,56},{56,64},{64,7... | collective-permute-start | bytes 1769480 | tf_op jit(solution)/shard_map/ppermute | solution.py:15
  184.0 154.5 %collective-permute-start.5 = (bf16[1,128,24,96]{1,3,2,0:T(8,128)(2,1)}, bf16[1,128,24,96]{1,3,2,0:T(8,128)(2,1)}, u32[]{:S(2)}, u32[]{:S(2)}) collective-permute-start(bf16[1,128,24,96]{1,3,2,0:T(8,128)(2,1)} %copy.72), channel_id=1, source_target_pairs={{8,0},{16,8},{24,16},{32,24},{40,32},{48,40},{56,48},{64,56},{72,6... | collective-permute-start | bytes 1769480 | tf_op jit(solution)/shard_map/ppermute | solution.py:17
  340.9 6.3 %copy-start.22 = (bf16[1,128,24,96]{3,2,1,0:T(8,128)(2,1)S(1)}, bf16[1,128,24,96]{3,2,1,0:T(8,128)(2,1)}, u32[]{:S(2)}) copy-start(bf16[1,128,24,96]{3,2,1,0:T(8,128)(2,1)} %copy.74) | copy-start | bytes 1769476
  341.7 6.1 %collective-permute-start.7 = (bf16[4,1,24,96]{3,2,1,0:T(8,128)(2,1)S(1)}, bf16[4,1,24,96]{3,2,1,0:T(8,128)(2,1)S(1)}, u32[]{:S(2)}, u32[]{:S(2)}) collective-permute-start(bf16[4,1,24,96]{3,2,1,0:T(8,128)(2,1)S(1)} %get-tuple-element.36), channel_id=1, source_target_pairs={{0,1},{1,2},{2,3},{3,4},{4,5},{5,6},{6,7},{8,9},{9,10},{10,11},{11... | collective-permute-start | bytes 55304 | tf_op jit(solution)/shard_map/ppermute | solution.py:15
  345.2 5.1 %collective-permute-start.6 = (bf16[4,1,24,96]{3,2,1,0:T(8,128)(2,1)S(1)}, bf16[4,1,24,96]{3,2,1,0:T(8,128)(2,1)S(1)}, u32[]{:S(2)}, u32[]{:S(2)}) collective-permute-start(bf16[4,1,24,96]{3,2,1,0:T(8,128)(2,1)S(1)} %get-tuple-element.37), channel_id=1, source_target_pairs={{1,0},{2,1},{3,2},{4,3},{5,4},{6,5},{7,6},{9,8},{10,9},{11,10},{12... | collective-permute-start | bytes 55304 | tf_op jit(solution)/shard_map/ppermute | solution.py:17
  353.5 1.7 copy-start.3
  353.5 1.7 copy-start.28
  359.6 1.7 copy-start.37
  362.4 1.0 copy-start.26
  362.4 1.4 copy-start.33
  431.9 2.7 copy-start.1
  (1 other events, 0.7 us)
Sparse Core Ops, SparseCore 0:
  188.2 147.0 all-reduce.4
where the time goes:
time: 449 us; the launch traced here: 442 us
  waiting for transfers between devices  175 us (39%)
  local copies, waits for them, and re-layouts  75 us (17%)
  blocking collectives  64.4 us (14%)
  starting transfers between devices  43.2 us (10%)
  other arithmetic  40.4 us (9%)
  matrix products  28.8 us (6%)
  between operations  15.3 us (3%)
    psum x1, waiting for transfers between devices, shards(): lax.psum((grad_a, grad_b, grad_h), ('patch', 'body'))  145 us
    psum x1, blocking collectives, shards(): lax.psum((grad_a, grad_b, grad_h), ('patch', 'body'))  64.4 us
    scatter-add x1, other arithmetic, shards(): summed = jnp.zeros((points, width), jnp.float32).at[inslot.reshape(-1)].a...  24 us
    all_to_all x1, waiting for transfers between devices, shards(): lax.all_to_all(outbox.reshape(width, n_dev, cap), ('patch', 'body'), spli...  17.7 us
    ppermute x4, starting transfers between devices, with_halo(): lax.ppermute(tail, axis, [(i, (i + 1) % count) for i in range(ends)])  16.2 us
    all_to_all x1, starting transfers between devices, shards(): lax.all_to_all(outslot.reshape(1, n_dev, cap), ('patch', 'body'), split_a...  11.5 us
    unnamed x80, local copies, waits for them, and re-layouts  11.5 us
  transfers between devices with their start and end apart: 11, of which 6 were waited for; matrix products, arithmetic and copies ran while one was open for 6% of the time, Pallas kernels for 0%

commit v1 on v0

v1 whole, which is shorter than its diff:
```python
import functools

import jax
import jax.numpy as jnp
from jax import lax
from jax.experimental import pallas as pl
from jax.experimental.pallas import tpu as pltpu
from jax.sharding import PartitionSpec as P

F32 = jnp.float32
BF16 = jnp.bfloat16
AXES = ("patch", "body")
C = 96
H = 24
F = 5
V = H * F
TX = 2
TY = 128
S = TY + 4
Q = 896
LO, HI = 128, 768
OLO, OHI = 256, 640
NA = HI - LO
NO = OHI - OLO
OWN = (2 * S + 2, 3 * S + 2)
TAPS = tuple((di - 1) * S + (dj - 1) for di in range(3) for dj in range(3))
KB = 9 * C
COLS = (((1,), (1,)), ((), ()))
LIMIT = 60 * 1024 * 1024


def dot(a, b):
    return jnp.dot(a, b, preferred_element_type=F32)


def dot_t(a, b):
    return lax.dot_general(a, b, COLS, preferred_element_type=F32)


def iota(shape, dim):
    return lax.broadcasted_iota(jnp.int32, shape, dim)


def pack_kernel(cap, donors, owner, slot, out, dext, place):
    rows = donors.shape[1]
    n_dev = 128
    dext[0:V, :] = donors[...]
    pad = iota((8, rows), 0)
    dext[V : V + 8, :] = jnp.where(pad == 0, slot[...], 0).astype(F32).astype(BF16)
    wide = 256
    upper = (iota((wide, wide), 0) < iota((wide, wide), 1)).astype(F32).astype(BF16)
    carry = jnp.zeros((n_dev, 1), F32)
    for at in range(0, rows, wide):
        dest = owner[:, at : at + wide]
        hit = (iota((n_dev, wide), 0) == dest).astype(F32)
        before = dot(hit.astype(BF16), upper) + carry
        rank = jnp.sum(before * hit, axis=0, keepdims=True)
        carry = carry + jnp.sum(hit, axis=1, keepdims=True)
        place[:, at : at + wide] = dest * cap + rank.astype(jnp.int32)
    block = 256

    def step(n, _):
        base = n * block
        pick = (iota((block, rows), 0) == place[...] - base).astype(F32).astype(BF16)
        out[pl.ds(pl.multiple_of(base, block), block), :] = dot_t(pick, dext[...]).astype(BF16)
        return 0

    lax.fori_loop(0, n_dev * cap // block, step, 0)


def unpack_kernel(inbox, target, prof, left, right, side):
    total = inbox.shape[0]
    points = TX * TY
    lane = iota((8, 128), 1)
    mark = (lane == V).astype(F32).astype(BF16)
    acc = jnp.zeros((points, 128), F32)
    chunk = 1024
    for at in range(0, total, chunk):
        rows = inbox[at : at + chunk, :]
        slots = dot_t(mark, rows)[0:1, :].astype(jnp.int32)
        pick = (iota((points, chunk), 0) == slots).astype(F32).astype(BF16)
        acc = acc + dot(pick, rows)
    acc = jnp.where(iota((points, 128), 1) < V, acc, 0.0)
    for r in range(TX):
        goal = target[:, r, :]
        high = goal.astype(BF16).astype(F32)
        rest = goal - high
        side[...] = jnp.zeros((128, 128), F32)
        side[V : V + 3, :] = high
        side[V + 3 : V + 6, :] = rest
        part = acc[r * TY : (r + 1) * TY, :] + jnp.transpose(side[...])
        prof[r * TY : (r + 1) * TY, :] = part.astype(BF16)
        if r == 0:
            keep = part
    side[0:2, :] = keep[0:2, :]
    side[2:4, :] = part[0:2, :]
    side[4:16, :] = jnp.zeros((12, 128), F32)
    left[...] = side[0:16, :].astype(BF16)
    side[0:2, :] = keep[TY - 2 : TY, :]
    side[2:4, :] = part[TY - 2 : TY, :]
    right[...] = side[0:16, :].astype(BF16)


def step_kernel(own, upper, lower, wa, wat, wf, wb, wh, wht, sel, stress_out, pgrad, grads,
                ext, prof, unf, zc, u1s, u2s, z2s, dac, da1s, err_s, gb):
    ext[S * 6 : Q, :] = jnp.zeros((Q - S * 6, 128), F32)
    for row, src in ((0, upper), (2, own), (4, lower)):
        block = src[...].astype(F32)
        for r in range(TX):
            at = (row + r) * S
            ext[at : at + 2, :] = block[256 + 2 * r : 258 + 2 * r, :]
            ext[at + 2 : at + 2 + TY, :] = block[r * TY : (r + 1) * TY, :]
            ext[at + 2 + TY : at + S, :] = block[272 + 2 * r : 274 + 2 * r, :]
    wide = jnp.transpose(ext[...])
    prof[...] = wide.astype(BF16)
    goal = wide[V : V + 8, LO:HI]
    goal = goal + jnp.concatenate([goal[3:8], goal[0:3]], axis=0)

    lane = iota((8, NA), 1) + LO
    row_at = lane // S
    col_at = lane - row_at * S
    grid_x = lax.axis_index("patch") * TX + row_at - 2
    grid_y = lax.axis_index("body") * TY + col_at - 2
    width_x = lax.axis_size("patch") * TX
    width_y = lax.axis_size("body") * TY
    ring = (row_at >= 1) & (row_at <= 4) & (col_at >= 1) & (col_at <= S - 2)
    inside = (grid_x >= 0) & (grid_x < width_x) & (grid_y >= 0) & (grid_y < width_y)
    mine = (row_at >= 2) & (row_at <= 3) & (col_at >= 2) & (col_at <= S - 3)
    ring_mask = (ring & inside & (iota((8, NA), 0) < 3)).astype(F32)
    own_mask = mine.astype(F32)

    def forward(h, _):
        u1 = dot(wa[h], prof[...])
        z1f = u1 + u1 * jnp.tanh(u1)
        z1 = z1f.astype(BF16)
        u1s[h] = u1[:, OLO:OHI]
        z1c = z1f.astype(BF16).astype(F32)
        for tap, shift in enumerate(TAPS):
            moved = z1c if shift == 0 else pltpu.roll(z1c, (-shift) % Q, 1)
            zc[h, tap * C : (tap + 1) * C, :] = moved[:, LO:HI].astype(BF16)
        u2 = dot(wf[...], zc[h])
        u2s[h] = u2
        act = z1c[:, LO:HI] + (u2 + u2 * jnp.tanh(u2))
        z2s[h] = act.astype(BF16)
        return 0

    lax.fori_loop(0, H, forward, 0)
    z2 = z2s[...].reshape(H * C, NA)
    stress = dot(wh[...], z2)
    for r in range(TX):
        at = OWN[r] - LO
        stress_out[:, r, :] = stress[0:3, at : at + TY]
    err = ((stress - goal) * ring_mask).astype(BF16)
    err_s[...] = err
    err_own = (err[:, OLO - LO : OHI - LO].astype(F32) * own_mask[:, OLO - LO : OHI - LO]).astype(BF16)
    grad_h = dot_t(err_own, z2s[:, :, OLO - LO : OHI - LO].reshape(H * C, NO))
    for t in range(H * C // 128):
        grads[108 + t] = grad_h[:, t * 128 : (t + 1) * 128]
    own_wide = jnp.broadcast_to(own_mask[0:1, OLO - LO : OHI - LO], (C, NO))
    own_prof = (prof[:, OLO:OHI].astype(F32) * own_mask[0:1, OLO - LO : OHI - LO]).astype(BF16)
    unf[...] = dot(sel[...], own_prof).astype(BF16).reshape(H, 16, NO)
    gb[...] = jnp.zeros_like(gb)

    def backward(h, grad_a):
        u2 = u2s[h]
        t2 = jnp.tanh(u2)
        dz2 = dot(wht[h], err_s[...])
        da2 = (dz2 * ((1.0 + t2) * (1.0 + u2 * (1.0 - t2)))).astype(BF16)
        da2f = da2.astype(F32)
        mid = (da2f[:, OLO - LO : OHI - LO] * own_wide).astype(BF16)
        gb[...] += dot_t(mid, zc[h, :, OLO - LO : OHI - LO])
        for tap, shift in enumerate(TAPS):
            moved = da2f if shift == 0 else pltpu.roll(da2f, shift % NA, 1)
            dac[tap * C : (tap + 1) * C, :] = moved[:, OLO - LO : OHI - LO].astype(BF16)
        dz1 = dz2[:, OLO - LO : OHI - LO] + dot(wb[...], dac[...])
        u1 = u1s[h]
        t1 = jnp.tanh(u1)
        da1 = (dz1 * ((1.0 + t1) * (1.0 + u1 * (1.0 - t1)))).astype(BF16)
        da1s[h] = da1
        return grad_a + dot_t(unf[h], da1)

    grad_a = lax.fori_loop(0, H, backward, jnp.zeros((16, C), F32))
    blank = jnp.zeros((16, 128 - C), F32)
    grad_a = jnp.concatenate([grad_a, blank], axis=1)
    grads[126] = grad_a[0:8]
    grads[127] = grad_a[8:16]
    grad_b = jnp.transpose(gb[...])
    blank = jnp.zeros((KB, 128 - C), F32)
    grads[0:108] = jnp.concatenate([grad_b, blank], axis=1).reshape(108, 8, 128)
    back = dot(wat[...], da1s[...].reshape(H * C, NO))
    for r in range(TX):
        at = OWN[r] - OLO
        pgrad[:, r, :] = back[0:V, at : at + TY]


def spread_kernel(sums, grad_a, grad_b, grad_h):
    for tap in range(9):
        rows = sums[12 * tap : 12 * (tap + 1)].astype(F32).reshape(C, 128)
        grad_b[tap] = rows[:, 0:C]
    for t in range(H * C // 128):
        grad_h[:, t * 128 : (t + 1) * 128] = sums[108 + t].astype(F32)[0:3]
    low = sums[126].astype(F32)[:, 0:C]
    high = sums[127].astype(F32)[:, 0:C]
    for k in range(3):
        for f in range(F):
            n = k * F + f
            grad_a[f, k : k + 1, :] = low[n : n + 1] if n < 8 else high[n - 8 : n - 7]


def call(kernel, out_shape, scratch=()):
    return pl.pallas_call(
        kernel,
        out_shape=out_shape,
        scratch_shapes=list(scratch),
        compiler_params=pltpu.CompilerParams(vmem_limit_bytes=LIMIT),
    )


def shape(dims, kind):
    return jax.ShapeDtypeStruct(dims, kind)


def exchange(blocks):
    return lax.all_to_all(blocks, AXES, split_axis=0, concat_axis=0, tiled=True)


def shards(donors, owner, slot, target, weight_a, weight_b, weight_h):
    n_patch = lax.axis_size("patch")
    n_body = lax.axis_size("body")
    n_dev = n_patch * n_body
    rows = donors.shape[1]
    cap = 2 * rows // n_dev
    outbox = call(
        functools.partial(pack_kernel, cap),
        shape((n_dev * cap, 128), BF16),
        [pltpu.VMEM((128, rows), BF16), pltpu.VMEM((1, rows), jnp.int32)],
    )(donors, owner.reshape(1, rows), slot.reshape(1, rows))
    inbox = exchange(outbox.reshape(n_dev, cap, 128)).reshape(n_dev * cap, 128)

    half = jnp.asarray(0.5, BF16)
    heights = jnp.arange(H)
    reach = heights[None, :, None] + 2 * (jnp.arange(3)[:, None, None] - 1) == heights[None, None, :]
    band = jnp.einsum("khg,kfc->hcgf", reach.astype(BF16), weight_a).reshape(H * C, V)
    band = jnp.pad(band, ((0, 0), (0, 128 - V)))
    wa = (band * half).reshape(H, C, 128)
    wat = jnp.transpose(band)
    wf = jnp.transpose(weight_b, (2, 0, 1)).reshape(C, KB) * half
    wb = jnp.transpose(weight_b, (1, 0, 2)).reshape(C, KB) * half
    wh = jnp.pad(jnp.transpose(weight_h), ((0, 5), (0, 0)))
    wht = (jnp.pad(weight_h, ((0, 0), (0, 5))) * half).reshape(H, C, 8)
    line = jnp.arange(16)
    want = (heights[:, None] + 2 * (line[None, :] // F - 1)) * F + line[None, :] % F
    sel = (want[:, :, None] == jnp.arange(128)[None, None, :]) & (want >= 0)[:, :, None]
    sel = sel & (want < V)[:, :, None] & (line < 15)[None, :, None]
    sel = sel.astype(BF16).reshape(H * 16, 128)

    prof, left, right = call(
        unpack_kernel,
        (shape((TX * TY, 128), BF16), shape((16, 128), BF16), shape((16, 128), BF16)),
        [pltpu.VMEM((128, 128), F32)],
    )(inbox, jnp.transpose(target, (2, 0, 1)))
    fore = [(i, i + 1) for i in range(n_body - 1)]
    back = [(i + 1, i) for i in range(n_body - 1)]
    from_left = lax.ppermute(right, "body", fore)
    from_right = lax.ppermute(left, "body", back)
    tile = jnp.concatenate([prof, from_left, from_right], axis=0)
    fore = [(i, i + 1) for i in range(n_patch - 1)]
    back = [(i + 1, i) for i in range(n_patch - 1)]
    above = lax.ppermute(tile, "patch", fore)
    below = lax.ppermute(tile, "patch", back)

    stress, pgrad, grads = call(
        step_kernel,
        (shape((3, TX, TY), F32), shape((V, TX, TY), F32), shape((128, 8, 128), F32)),
        [
            pltpu.VMEM((Q, 128), F32),
            pltpu.VMEM((128, Q), BF16),
            pltpu.VMEM((H, 16, NO), BF16),
            pltpu.VMEM((H, KB, NA), BF16),
            pltpu.VMEM((H, C, NO), F32),
            pltpu.VMEM((H, C, NA), F32),
            pltpu.VMEM((H, C, NA), BF16),
            pltpu.VMEM((KB, NO), BF16),
            pltpu.VMEM((H, C, NO), BF16),
            pltpu.VMEM((8, NA), BF16),
            pltpu.VMEM((C, KB), F32),
        ],
    )(tile, above, below, wa, wat, wf, wb, wh, wht, sel)
    scale = 1.0 / jnp.sqrt(jnp.float32(TX * TY * n_dev))
    total = (jnp.sum(exchange(grads), axis=0) * scale).astype(BF16)
    sums = exchange(jnp.broadcast_to(total[None], (n_dev, 8, 128)))
    grad_a, grad_b, grad_h = call(
        spread_kernel,
        (shape((F, 3, C), F32), shape((9, C, C), F32), shape((3, H * C), F32)),
    )(sums)
    return (
        jnp.transpose(stress, (1, 2, 0)),
        pgrad,
        jnp.transpose(grad_a, (1, 0, 2)),
        grad_b,
        jnp.transpose(grad_h),
    )


def solution(mesh):
    placed = (
        P(None, ("patch", "body")),
        P(("patch", "body"), None),
        P(("patch", "body")),
        P("patch", "body", None),
        P(),
        P(),
        P(),
    )
    return jax.shard_map(
        shards,
        mesh=mesh,
        in_specs=placed,
        out_specs=(P("patch", "body", None), P(None, "patch", "body"), P(), P(), P()),
        check_vma=False,
    )
```

time: 449 us -> 143 us (0.32); the launches traced: 442 us -> 143 us
  waiting for transfers between devices: 175 us -> 19.4 us
  local copies, waits for them, and re-layouts: 75 us -> 8.37 us
  Pallas kernels: 0 us -> 55.2 us
  other arithmetic: 40.4 us -> 2.05 us
  matrix products: 28.8 us -> 0.69 us
  blocking collectives: 64.4 us -> 37.3 us
  starting transfers between devices: 43.2 us -> 19 us
  between operations: 15.3 us -> 0.83 us
    psum x1 -> x0, waiting for transfers between devices: 145 us -> none  [shards(): lax.psum((grad_a, grad_b, grad_h), ('patch', 'body'))]
    psum x1 -> x0, blocking collectives: 64.4 us -> none  [shards(): lax.psum((grad_a, grad_b, grad_h), ('patch', 'body'))]
    pallas_call x0 -> x4, Pallas kernels: none -> 55.2 us  [the longest x1 41 us: shards(): call(step_kernel, (shape((3, TX, TY), F32), shape((V, TX, TY), F32), shap...]
    all_to_all x0 -> x2, blocking collectives: none -> 37.3 us  [exchange(): return lax.all_to_all(blocks, AXES, split_axis=0, concat_axis=0, tiled=True)]
    dot_general x35 -> x1, matrix products: 28.8 us -> 0.69 us  [shards(): jnp.einsum('khg,kfc->hcgf', reach.astype(BF16), weight_a).reshape(H * C, V)]
    scatter-add x1 -> x0, other arithmetic: 24 us -> none  [shards(): summed = jnp.zeros((points, width), jnp.float32).at[inslot.reshape(-1)].a...]
    slice x17 -> x0, local copies, waits for them, and re-layouts: 19.2 us -> none  [the longest x5 8.29 us: with_halo(): head = lax.slice_in_dim(cells, 0, width, axis=dim)]
    ppermute x8 -> x4, starting transfers between devices: 24.3 us -> 7.53 us  [the longest x1 3.05 us: shards(): from_left = lax.ppermute(right, 'body', fore)]
  transfers between devices with their start and end apart: 11 -> 5, of which waited for: 6 -> 2; matrix products, arithmetic and copies ran while one was open for 6% -> 6% of each run, Pallas kernels for 0% -> 0%
where the time goes in v1:
time: 143 us
  Pallas kernels  55.2 us (39%)
  blocking collectives  37.3 us (26%)
  waiting for transfers between devices  19.4 us (14%)
  starting transfers between devices  19 us (13%)
  local copies, waits for them, and re-layouts  8.37 us (6%)
  other arithmetic  2.05 us (1%)
    pallas_call x1, Pallas kernels, shards(): call(step_kernel, (shape((3, TX, TY), F32), shape((V, TX, TY), F32), shap...  41 us
    all_to_all x2, blocking collectives, exchange(): return lax.all_to_all(blocks, AXES, split_axis=0, concat_axis=0, tiled=True)  37.3 us
    all_to_all x1, waiting for transfers between devices, exchange(): return lax.all_to_all(blocks, AXES, split_axis=0, concat_axis=0, tiled=True)  16.2 us
    all_to_all x1, starting transfers between devices, exchange(): return lax.all_to_all(blocks, AXES, split_axis=0, concat_axis=0, tiled=True)  11.5 us
    pallas_call x1, Pallas kernels, shards(): call(functools.partial(pack_kernel, cap), shape((n_dev * cap, 128), BF16)...  9.47 us
    ppermute x1, waiting for transfers between devices, shards(): from_right = lax.ppermute(left, 'body', back)  3.19 us
    ppermute x1, starting transfers between devices, shards(): from_left = lax.ppermute(right, 'body', fore)  3.05 us
    pallas_call x1, Pallas kernels, shards(): call(unpack_kernel, (shape((TX * TY, 128), BF16), shape((16, 128), BF16),...  3.05 us
  transfers between devices with their start and end apart: 5, of which 2 were waited for; matrix products, arithmetic and copies ran while one was open for 6% of the time, Pallas kernels for 0%

profile of v1, /device:TPU:1, one launch (start us, length us, event | category | flops | bytes accessed | tf_op | source)
XLA Modules:
  0.0 142.8 jit_solution(10694523961338695412)
XLA Ops:
  0.6 0.0 copy-start
  0.6 9.5 %shard_map.110 = bf16[4096,128]{1,0:T(8,128)(2,1)} custom-call(bf16[120,2048]{1,0:T(8,128)(2,1)} %donors.1, s32[1,2048]{1,0:T(1,128)} %bitcast.44, s32[1,2048]{1,0:T(1,128)} %bitcast.45), custom_call_target="tpu_custom_call" | custom-call | tf_op jit(solution)/shard_map/pallas_call | solution.py:233
  10.1 11.5 %all-to-all-start = ((bf16[128,32,128]{2,1,0:T(8,128)(2,1)}), bf16[128,32,128]{2,1,0:T(8,128)(2,1)S(1)}, u32[]{:S(2)}, u32[]{:S(2)}) async-start(bf16[128,32,128]{2,1,0:T(8,128)(2,1)} %bitcast.38), calls=%async_computation | async-start | bytes 2097152 | tf_op jit(solution)/shard_map/all_to_all | solution.py:224
  21.7 0.1 add.106
  21.7 0.1 add.110
  21.8 0.1 add.104
  22.0 0.0 copy-done
  22.0 0.7 convolution_bitcast_fusion
  22.7 0.1 and.56
  22.8 0.0 copy-start.3
  22.8 0.1 copy.17
  22.9 0.0 copy-start.6
  22.9 0.6 reshape.210
  23.5 0.2 copy-done.3
  23.7 0.0 copy-done.6
  23.8 0.9 pad_bitcast_fusion
  24.7 16.2 %all-to-all-done = bf16[128,32,128]{2,1,0:T(8,128)(2,1)S(1)} async-done(((bf16[128,32,128]{2,1,0:T(8,128)(2,1)}), bf16[128,32,128]{2,1,0:T(8,128)(2,1)S(1)}, u32[]{:S(2)}, u32[]{:S(2)}) %all-to-all-start) | async-done | bytes 1048608 | tf_op jit(solution)/shard_map/all_to_all | solution.py:224
  40.8 0.0 copy-start.1
  40.8 1.0 copy-done.1
  41.8 3.0 %shard_map.111 = (bf16[256,128]{1,0:T(8,128)(2,1)}, bf16[16,128]{1,0:T(8,128)(2,1)}, bf16[16,128]{1,0:T(8,128)(2,1)}) custom-call(bf16[4096,128]{1,0:T(8,128)(2,1)} %bitcast.37, f32[3,2,128]{2,1,0:T(2,128)} %bitcast.46), custom_call_target="tpu_custom_call" | custom-call | tf_op jit(solution)/shard_map/pallas_call | solution.py:257
  44.9 3.0 %collective-permute-start = (bf16[16,128]{1,0:T(8,128)(2,1)}, bf16[16,128]{1,0:T(8,128)(2,1)S(1)}, u32[]{:S(2)}, u32[]{:S(2)}) collective-permute-start(bf16[16,128]{1,0:T(8,128)(2,1)} %get-tuple-element.15), channel_id=1, source_target_pairs={{0,1},{1,2},{2,3},{3,4},{4,5},{5,6},{6,7},{8,9},{9,10},{10,11},{11... | collective-permute-start | bytes 12296 | tf_op jit(solution)/shard_map/ppermute | solution.py:264
  47.9 0.8 constant_dynamic-update-slice_fusion.2
  48.8 1.9 %collective-permute-start.1 = (bf16[16,128]{1,0:T(8,128)(2,1)}, bf16[16,128]{1,0:T(8,128)(2,1)S(1)}, u32[]{:S(2)}, u32[]{:S(2)}) collective-permute-start(bf16[16,128]{1,0:T(8,128)(2,1)} %get-tuple-element.16), channel_id=1, source_target_pairs={{1,0},{2,1},{3,2},{4,3},{5,4},{6,5},{7,6},{9,8},{10,9},{11,10},{12... | collective-permute-start | bytes 12296 | tf_op jit(solution)/shard_map/ppermute | solution.py:265
  50.7 0.0 collective-permute-done
  50.7 3.2 %collective-permute-done.1 = bf16[16,128]{1,0:T(8,128)(2,1)S(1)} collective-permute-done((bf16[16,128]{1,0:T(8,128)(2,1)}, bf16[16,128]{1,0:T(8,128)(2,1)S(1)}, u32[]{:S(2)}, u32[]{:S(2)}) %collective-permute-start.1) | collective-permute-done | bytes 4128 | tf_op jit(solution)/shard_map/ppermute | solution.py:265
  53.9 0.0 copy-start.2
  53.9 1.3 collective-permute-start.2
  55.2 1.3 collective-permute-start.3
  56.5 0.9 fusion.3.sel
  57.4 1.1 copy.18
  58.5 0.2 copy.19
  58.7 0.8 copy.22.wb
  59.5 0.0 copy-done.2
  59.5 0.8 copy.21.wf
  60.3 1.1 copy.20
  61.4 0.6 pad.13.wh
  62.0 0.0 collective-permute-done.2.upper
  62.0 0.0 copy-start.4
  62.0 0.0 collective-permute-done.3.lower
  62.0 0.0 copy-start.5
  62.0 0.6 copy-done.4
  62.6 0.0 copy-done.5
  62.6 41.0 %shard_map.112 = (f32[3,2,128]{2,1,0:T(2,128)}, f32[120,2,128]{2,1,0:T(2,128)}, f32[128,8,128]{2,1,0:T(8,128)}) custom-call(bf16[288,128]{1,0:T(8,128)(2,1)} %copy-done.2, bf16[288,128]{1,0:T(8,128)(2,1)} %copy-done.4, bf16[288,128]{1,0:T(8,128)(2,1)} %copy-done.5, bf16[24,96,128]{2,1,0:T(8,128)(2,1)} %bitcast.39, bf16[128,2304]{1,0:T(8,128)(2,1)} %get-tuple-element.25.wat, ...), custom_call_target="tpu_custom_call" | custom-call | tf_op jit(solution)/shard_map/pallas_call | solution.py:272
  103.6 21.7 %all_to_all.15 = f32[128,8,128]{2,1,0:T(8,128)S(1)} all-to-all(f32[128,8,128]{2,1,0:T(8,128)} %get-tuple-element.19), channel_id=1, replica_groups=mesh['patch'=16,'body'=8] {'patch','body'}, dimensions={0} | all-to-all | bytes 1048576 | tf_op jit(solution)/shard_map/all_to_all | solution.py:224
  125.3 0.1 reduce_sum.9
  125.5 15.6 %all_to_all.16.sums = bf16[128,8,128]{2,1,0:T(8,128)(2,1)} all-to-all(bf16[128,8,128]{2,1,0:T(8,128)(2,1)S(1)} %broadcast_in_dim.2), channel_id=1, replica_groups=mesh['patch'=16,'body'=8] {'patch','body'}, dimensions={0} | all-to-all | bytes 524288 | tf_op jit(solution)/shard_map/all_to_all | solution.py:224
  141.1 1.7 %shard_map.113 = (f32[5,3,96]{2,1,0:T(4,128)}, f32[9,96,96]{2,1,0:T(8,128)}, f32[3,2304]{1,0:T(4,128)}) custom-call(bf16[128,8,128]{2,1,0:T(8,128)(2,1)} %all_to_all.16.sums), custom_call_target="tpu_custom_call" | custom-call | tf_op jit(solution)/shard_map/pallas_call | solution.py:292
  (17 shorter events, 0.2 us)
Async XLA Ops:
  0.6 21.3 %copy-start = (bf16[3,5,96]{2,0,1:T(4,128)(2,1)S(1)}, bf16[3,5,96]{2,0,1:T(4,128)(2,1)}, u32[]{:S(2)}) copy-start(bf16[3,5,96]{2,0,1:T(4,128)(2,1)} %param.11) | copy-start | bytes 8644
  10.1 30.7 %all-to-all-start = ((bf16[128,32,128]{2,1,0:T(8,128)(2,1)}), bf16[128,32,128]{2,1,0:T(8,128)(2,1)S(1)}, u32[]{:S(2)}, u32[]{:S(2)}) async-start(bf16[128,32,128]{2,1,0:T(8,128)(2,1)} %bitcast.38), calls=%async_computation | async-start | bytes 2097152 | tf_op jit(solution)/shard_map/all_to_all | solution.py:224
  22.8 0.9 copy-start.3
  22.9 0.9 copy-start.6
  40.8 1.0 copy-start.1
  44.9 5.8 %collective-permute-start = (bf16[16,128]{1,0:T(8,128)(2,1)}, bf16[16,128]{1,0:T(8,128)(2,1)S(1)}, u32[]{:S(2)}, u32[]{:S(2)}) collective-permute-start(bf16[16,128]{1,0:T(8,128)(2,1)} %get-tuple-element.15), channel_id=1, source_target_pairs={{0,1},{1,2},{2,3},{3,4},{4,5},{5,6},{6,7},{8,9},{9,10},{10,11},{11... | collective-permute-start | bytes 12296 | tf_op jit(solution)/shard_map/ppermute | solution.py:264
  48.8 5.1 %collective-permute-start.1 = (bf16[16,128]{1,0:T(8,128)(2,1)}, bf16[16,128]{1,0:T(8,128)(2,1)S(1)}, u32[]{:S(2)}, u32[]{:S(2)}) collective-permute-start(bf16[16,128]{1,0:T(8,128)(2,1)} %get-tuple-element.16), channel_id=1, source_target_pairs={{1,0},{2,1},{3,2},{4,3},{5,4},{6,5},{7,6},{9,8},{10,9},{11,10},{12... | collective-permute-start | bytes 12296 | tf_op jit(solution)/shard_map/ppermute | solution.py:265
  53.9 5.6 %copy-start.2 = (bf16[288,128]{1,0:T(8,128)(2,1)}, bf16[288,128]{1,0:T(8,128)(2,1)S(1)}, u32[]{:S(2)}) copy-start(bf16[288,128]{1,0:T(8,128)(2,1)S(1)} %constant_dynamic-update-slice_fusion.own) | copy-start | bytes 221188
  53.9 8.1 %collective-permute-start.2 = (bf16[288,128]{1,0:T(8,128)(2,1)S(1)}, bf16[288,128]{1,0:T(8,128)(2,1)S(1)}, u32[]{:S(2)}, u32[]{:S(2)}) collective-permute-start(bf16[288,128]{1,0:T(8,128)(2,1)S(1)} %constant_dynamic-update-slice_fusion.own), channel_id=1, source_target_pairs={{0,8},{8,16},{16,24},{24,32},{32,40},{40,48},{48,56},{56,64},{64,7... | collective-permute-start | bytes 221192 | tf_op jit(solution)/shard_map/ppermute | solution.py:269
  55.2 6.8 %collective-permute-start.3 = (bf16[288,128]{1,0:T(8,128)(2,1)S(1)}, bf16[288,128]{1,0:T(8,128)(2,1)S(1)}, u32[]{:S(2)}, u32[]{:S(2)}) collective-permute-start(bf16[288,128]{1,0:T(8,128)(2,1)S(1)} %constant_dynamic-update-slice_fusion.own), channel_id=1, source_target_pairs={{8,0},{16,8},{24,16},{32,24},{40,32},{48,40},{56,48},{64,56},{72,6... | collective-permute-start | bytes 221192 | tf_op jit(solution)/shard_map/ppermute | solution.py:270
  62.0 0.6 copy-start.4
  62.0 0.7 copy-start.5

commit v2 on v1

v2 whole, which is shorter than its diff:
```python
import functools

import jax
import jax.numpy as jnp
from jax import lax
from jax.experimental import pallas as pl
from jax.experimental.pallas import tpu as pltpu
from jax.sharding import PartitionSpec as P

F32 = jnp.float32
BF16 = jnp.bfloat16
AXES = ("patch", "body")
C = 96
H = 24
F = 5
V = H * F
TX = 2
TY = 128
ROWS = TX + 4
NZ = ROWS + 1
NA = ROWS - 1
Q = NZ * TY
KB = 9 * C
BESIDE = tuple((di - 1) * 8 + (dj - 1) * 2 for di in range(3) for dj in range(3))
COLS = (((1,), (1,)), ((), ()))
MIB = 1024 * 1024


def dot(a, b):
    return jnp.dot(a, b, preferred_element_type=F32)


def dot_t(a, b):
    return lax.dot_general(a, b, COLS, preferred_element_type=F32)


def iota(shape, dim):
    return lax.broadcasted_iota(jnp.int32, shape, dim)


def pack_kernel(cap, donors_far, owner_far, slot_far, out, dext, owner, slot, place, sems):
    rows = donors_far.shape[1]
    n_dev = 128
    own_copy = pltpu.make_async_copy(owner_far, owner, sems.at[0])
    slot_copy = pltpu.make_async_copy(slot_far, slot, sems.at[1])
    donor_copy = pltpu.make_async_copy(donors_far, dext.at[0:V], sems.at[2])
    own_copy.start()
    slot_copy.start()
    donor_copy.start()
    own_copy.wait()
    part = 256
    upper = (iota((part, part), 0) < iota((part, part), 1)).astype(F32).astype(BF16)
    carry = jnp.zeros((n_dev, 1), F32)
    spots = []
    for at in range(0, rows, part):
        dest = owner[:, at : at + part]
        hit = (iota((n_dev, part), 0) == dest).astype(F32)
        before = dot(hit.astype(BF16), upper) + carry
        rank = jnp.sum(before * hit, axis=0, keepdims=True)
        carry = carry + jnp.sum(hit, axis=1, keepdims=True)
        spot = (dest * cap).astype(F32) + rank
        spots += [spot[:, 0:128], spot[:, 128:256]]
    tall = jnp.transpose(jnp.concatenate(spots, axis=0))
    for n in range(rows // 128):
        place[n * 128 : (n + 1) * 128, :] = jnp.broadcast_to(tall[:, n : n + 1], (128, 128))
    slot_copy.wait()
    pad = iota((8, rows), 0)
    dext[V : V + 8, :] = jnp.where(pad == 0, slot[...], 0).astype(F32).astype(BF16)
    donor_copy.wait()
    block = 256
    marks = [(iota((1, 128), 1) + 128 * t).astype(F32).astype(BF16) for t in range(2)]

    one, none = jnp.asarray(1.0, BF16), jnp.asarray(0.0, BF16)

    def step(n, _):
        for m in range(2):
            base = (2 * n + m) * block
            spot = (place[...] - base.astype(F32)).astype(BF16)
            pick = jnp.concatenate([jnp.where(spot == mark, one, none) for mark in marks], axis=1)
            picked = dot(dext[...], pick)
            out[pl.ds(pl.multiple_of(base, block), block), :] = jnp.transpose(picked).astype(BF16)
        return 0

    lax.fori_loop(0, n_dev * cap // block // 2, step, 0)


def unpack_kernel(inbox, target, prof, left, right, side):
    total = inbox.shape[0]
    points = TX * TY
    lane = iota((8, 128), 1)
    mark = (lane == V).astype(F32).astype(BF16)
    acc = jnp.zeros((points, 128), F32)
    chunk = 1024
    for at in range(0, total, chunk):
        rows = inbox[at : at + chunk, :]
        slots = dot_t(mark, rows)[0:1, :].astype(jnp.int32)
        pick = (iota((points, chunk), 0) == slots).astype(F32).astype(BF16)
        acc = acc + dot(pick, rows)
    acc = jnp.where(iota((points, 128), 1) < V, acc, 0.0)
    for r in range(TX):
        goal = target[:, r, :]
        high = goal.astype(BF16).astype(F32)
        rest = goal - high
        side[...] = jnp.zeros((128, 128), F32)
        side[V : V + 3, :] = high
        side[V + 3 : V + 6, :] = rest
        part = acc[r * TY : (r + 1) * TY, :] + jnp.transpose(side[...])
        prof[r * TY : (r + 1) * TY, :] = part.astype(BF16)
        if r == 0:
            keep = part
    side[0:2, :] = keep[0:2, :]
    side[2:4, :] = part[0:2, :]
    side[4:16, :] = jnp.zeros((12, 128), F32)
    left[...] = side[0:16, :].astype(BF16)
    side[0:2, :] = keep[TY - 2 : TY, :]
    side[2:4, :] = part[TY - 2 : TY, :]
    right[...] = side[0:16, :].astype(BF16)


def turned(tile, shift):
    return tile if shift == 0 else pltpu.roll(tile, (-shift) % TY, 1)


def three(tile, beside, row):
    ends = turned(beside, 8 * row + 3)
    lane = iota((C, TY), 1)
    return (
        jnp.where(lane == 0, ends, turned(tile, -1)),
        tile,
        jnp.where(lane == TY - 1, ends, turned(tile, 1)),
    )


def wide_of(tiles):
    return jnp.concatenate(list(tiles), axis=1)


def step_kernel(own, first, second, wa, wat, wf, wb, wh, wht, sel, stress_out, pgrad, grads,
                ext, prof, unf, zs, zb, u1s, u2s, z2s, das, dzs, da1s, err_s, gb):
    patch = lax.axis_index("patch")
    body = lax.axis_index("body")
    odd_x = patch % 2 == 1
    odd_y = body % 2 == 1
    has_left = jnp.where(body > 0, 1.0, 0.0)
    has_right = jnp.where(body < lax.axis_size("body") - 1, 1.0, 0.0)
    has_up = jnp.where(patch > 0, 1.0, 0.0)
    has_down = jnp.where(patch < lax.axis_size("patch") - 1, 1.0, 0.0)
    ext[...] = jnp.zeros((128, 128), F32)
    goals = []
    one, two = first[...].astype(F32), second[...].astype(F32)
    sources = (
        jnp.where(odd_x, one, two) * has_up,
        own[...].astype(F32),
        jnp.where(odd_x, two, one) * has_down,
    )
    for row in range(ROWS):
        src, r = sources[row // TX], row % TX
        block = src[r * TY : (r + 1) * TY, :]
        one, two = src[256:288], src[288:320]
        left = jnp.where(odd_y, one, two)[16 + 2 * r : 18 + 2 * r] * has_left
        right = jnp.where(odd_y, two, one)[2 * r : 2 * r + 2] * has_right
        parts = (block[TY - 1 : TY], left[0:1], right[0:1], left[1:2], right[1:2], block[0:1])
        for n, part in enumerate(parts):
            ext[8 * row + n : 8 * row + n + 1, :] = part
        wide = jnp.transpose(block)
        prof[:, row * TY : (row + 1) * TY] = wide.astype(BF16)
        goals.append(wide[V : V + 8])
    wide = jnp.transpose(ext[...])
    prof[:, ROWS * TY : Q] = wide.astype(BF16)
    goal = wide_of(goals[1 : ROWS - 1] + [wide[V : V + 8]])
    goal = goal + jnp.concatenate([goal[3:8], goal[0:3]], axis=0)

    width = NA * TY
    lane = iota((8, width), 1)
    main = lane < (NA - 1) * TY
    spot = lane - (NA - 1) * TY
    row_at = jnp.where(main, lane // TY + 1, spot // 8)
    grid_x = patch * TX + row_at - TX
    inside_x = (grid_x >= 0) & (grid_x < lax.axis_size("patch") * TX)
    low = (spot % 8 == 3) & (body > 0)
    high = (spot % 8 == 2) & (body < lax.axis_size("body") - 1)
    ring = main | ((row_at >= 1) & (row_at <= ROWS - 2) & (low | high))
    mask = (ring & inside_x & (iota((8, width), 0) < 3)).astype(F32)

    def fill(zs_at, zb_at, p):
        for n in range(2):
            u1 = dot(wa[2 * p + n], prof[...])
            z1 = (u1 + u1 * jnp.tanh(u1)).astype(BF16)
            for r in range(TX):
                u1s[2 * p + n, r] = u1[:, (TX + r) * TY : (TX + r + 1) * TY]
            beside = z1[:, ROWS * TY : Q]
            for row in range(ROWS):
                for m, part in enumerate(three(z1[:, row * TY : (row + 1) * TY], beside, row)):
                    at = (3 * row + m) * C
                    zs_at[n, at : at + C, :] = part
            for tap, shift in enumerate(BESIDE):
                zb_at[n, tap * C : (tap + 1) * C, :] = turned(beside, shift)

    def wall(zs_at, zb_at, p):
        spots = [(n, t) for n in range(2) for t in range(NA)]

        def taps(n, t):
            return zb_at[n] if t == NA - 1 else zs_at[n, 3 * C * t : 3 * C * t + KB, :]

        for g in range(0, 2 * NA, 2):
            pair = spots[g : g + 2]
            both = dot(wf[...], wide_of([taps(n, t) for n, t in pair]))
            for m, (n, t) in enumerate(pair):
                u2 = both[:, TY * m : TY * (m + 1)]
                u2s[2 * p + n, t] = u2
                z1 = taps(n, t)[4 * C : 5 * C].astype(F32)
                act = z1 + (u2 + u2 * jnp.tanh(u2))
                rows = pl.ds(pl.multiple_of((2 * p + n) * C, C), C)
                z2s[t, rows, :] = act.astype(BF16)

    def forward(p, _):
        zs_at = zs.at[pl.ds(2 * p, 4)]
        zb_at = zb.at[pl.ds(2 * p, 4)]
        fill(zs_at.at[2:4], zb_at.at[2:4], p + 1)
        wall(zs_at.at[0:2], zb_at.at[0:2], p)
        return 0

    fill(zs.at[0:2], zb.at[0:2], 0)
    lax.fori_loop(0, H // 2 - 1, forward, 0)
    wall(zs.at[H - 2 : H], zb.at[H - 2 : H], H // 2 - 1)
    stress = wide_of(
        [dot(wh[...], wide_of([z2s[t] for t in range(n, min(n + 2, NA))])) for n in range(0, NA, 2)]
    )
    for r in range(TX):
        stress_out[:, r, :] = stress[0:3, (1 + r) * TY : (2 + r) * TY]
    err = ((stress - goal) * mask).astype(BF16)
    err_s[...] = err
    grad_h = dot_t(err[:, TY : 3 * TY], wide_of([z2s[1], z2s[2]]))
    for t in range(H * C // 128):
        grads[108 + t] = grad_h[:, t * 128 : (t + 1) * 128]
    unf[...] = dot(sel[...], prof[:, TX * TY : 2 * TX * TY]).astype(BF16).reshape(H, 16, TX * TY)
    gb[...] = jnp.zeros_like(gb)

    def third(das_at, dz_at, p):
        mids = []
        kept = []
        for n in range(2):
            h = 2 * p + n
            u2 = wide_of([u2s[h, t] for t in range(NA)])
            t2 = jnp.tanh(u2)
            dz2 = dot(wht[h], err_s[...])
            da2 = (dz2 * ((1.0 + t2) * (1.0 + u2 * (1.0 - t2)))).astype(BF16)
            beside = da2[:, (NA - 1) * TY : width]
            for t in range(NA - 1):
                for m, part in enumerate(three(da2[:, t * TY : (t + 1) * TY], beside, t + 1)):
                    at = (3 * t + m) * C
                    das_at[n, at : at + C, :] = part
            dz_at[n] = dz2[:, TY : 3 * TY]
            mids.append(da2[:, TY : 3 * TY])
            kept += [zs[h, 3 * C * t : 3 * C * t + KB, :] for t in (1, 2)]
        gb[...] += dot_t(wide_of(mids), wide_of(kept))

    def fourth(das_at, dz_at, p, grad_a):
        for n in range(2):
            h = 2 * p + n
            conv = dot(wb[...], wide_of([das_at[n, 3 * C * t : 3 * C * t + KB, :] for t in range(TX)]))
            u1 = wide_of([u1s[h, r] for r in range(TX)])
            t1 = jnp.tanh(u1)
            da1 = ((dz_at[n] + conv) * ((1.0 + t1) * (1.0 + u1 * (1.0 - t1)))).astype(BF16)
            rows = pl.ds(pl.multiple_of(h * C, C), C)
            for r in range(TX):
                da1s[r, rows, :] = da1[:, r * TY : (r + 1) * TY]
            grad_a = grad_a + dot_t(unf[h], da1)
        return grad_a

    def backward(p, grad_a):
        das_at = das.at[pl.ds(2 * p, 4)]
        dz_at = dzs.at[pl.ds(2 * p, 4)]
        third(das_at.at[2:4], dz_at.at[2:4], p + 1)
        return fourth(das_at.at[0:2], dz_at.at[0:2], p, grad_a)

    third(das.at[0:2], dzs.at[0:2], 0)
    grad_a = lax.fori_loop(0, H // 2 - 1, backward, jnp.zeros((16, C), F32))
    grad_a = fourth(das.at[H - 2 : H], dzs.at[H - 2 : H], H // 2 - 1, grad_a)
    blank = jnp.zeros((16, 128 - C), F32)
    grad_a = jnp.concatenate([grad_a, blank], axis=1)
    grads[126] = grad_a[0:8]
    grads[127] = grad_a[8:16]
    grad_b = jnp.transpose(gb[...])
    blank = jnp.zeros((KB, 128 - C), F32)
    grads[0:108] = jnp.concatenate([grad_b, blank], axis=1).reshape(108, 8, 128)
    back = dot(wat[...], wide_of([da1s[r] for r in range(TX)]))
    for r in range(TX):
        pgrad[:, r, :] = back[0:V, r * TY : (r + 1) * TY]


def spread_kernel(sums, grad_a, grad_b, grad_h):
    for tap in range(9):
        rows = sums[12 * tap : 12 * (tap + 1)].astype(F32).reshape(C, 128)
        grad_b[tap] = rows[:, 0:C]
    for t in range(H * C // 128):
        grad_h[:, t * 128 : (t + 1) * 128] = sums[108 + t].astype(F32)[0:3]
    low = sums[126].astype(F32)[:, 0:C]
    high = sums[127].astype(F32)[:, 0:C]
    for k in range(3):
        for f in range(F):
            n = k * F + f
            grad_a[f, k : k + 1, :] = low[n : n + 1] if n < 8 else high[n - 8 : n - 7]


def call(kernel, limit, out_shape, scratch=(), space=pltpu.VMEM):
    near = pl.BlockSpec(memory_space=pltpu.VMEM)

    def run(*operands):
        return pl.pallas_call(
            kernel,
            out_shape=out_shape,
            in_specs=[pl.BlockSpec(memory_space=space)] * len(operands),
            out_specs=jax.tree.map(lambda _: near, out_shape),
            scratch_shapes=list(scratch),
            compiler_params=pltpu.CompilerParams(vmem_limit_bytes=limit * MIB),
        )(*operands)

    return run


def shape(dims, kind):
    return jax.ShapeDtypeStruct(dims, kind)


def exchange(blocks):
    return lax.all_to_all(blocks, AXES, split_axis=0, concat_axis=0, tiled=True)


def trades(count):
    inner = [(i, i ^ 1) for i in range(count)]
    outer = [(i, i - 1 + 2 * (i % 2)) for i in range(1, count - 1)] + [(0, 0), (count - 1, count - 1)]
    return inner, outer


def shards(donors, owner, slot, target, weight_a, weight_b, weight_h):
    n_patch = lax.axis_size("patch")
    n_body = lax.axis_size("body")
    n_dev = n_patch * n_body
    rows = donors.shape[1]
    cap = 2 * rows // n_dev
    outbox = call(
        functools.partial(pack_kernel, cap),
        12,
        shape((n_dev * cap, 128), BF16),
        [
            pltpu.VMEM((128, rows), BF16),
            pltpu.VMEM((1, rows), jnp.int32),
            pltpu.VMEM((1, rows), jnp.int32),
            pltpu.VMEM((rows, n_dev), F32),
            pltpu.SemaphoreType.DMA((3,)),
        ],
        pltpu.HBM,
    )(donors, owner.reshape(1, rows), slot.reshape(1, rows))
    inbox = exchange(outbox.reshape(n_dev, cap, 128)).reshape(n_dev * cap, 128)

    half = jnp.asarray(0.5, BF16)
    heights = jnp.arange(H)
    reach = heights[None, :, None] + 2 * (jnp.arange(3)[:, None, None] - 1) == heights[None, None, :]
    band = jnp.einsum("khg,kfc->hcgf", reach.astype(BF16), weight_a).reshape(H * C, V)
    band = jnp.pad(band, ((0, 0), (0, 128 - V)))
    wa = (band * half).reshape(H, C, 128)
    wat = jnp.transpose(band)
    wf = jnp.transpose(weight_b, (2, 0, 1)).reshape(C, KB) * half
    wb = jnp.transpose(weight_b[::-1], (1, 0, 2)).reshape(C, KB) * half
    wh = jnp.pad(jnp.transpose(weight_h), ((0, 5), (0, 0)))
    wht = (jnp.pad(weight_h, ((0, 0), (0, 5))) * half).reshape(H, C, 8)
    line = jnp.arange(16)
    want = (heights[:, None] + 2 * (line[None, :] // F - 1)) * F + line[None, :] % F
    sel = (want[:, :, None] == jnp.arange(128)[None, None, :]) & (want >= 0)[:, :, None]
    sel = sel & (want < V)[:, :, None] & (line < 15)[None, :, None]
    sel = sel.astype(BF16).reshape(H * 16, 128)

    inbox, wa, wat, wf, wb, wh, wht, sel = lax.optimization_barrier(
        (inbox, wa, wat, wf, wb, wh, wht, sel)
    )
    prof, left, right = call(
        unpack_kernel,
        8,
        (shape((TX * TY, 128), BF16), shape((16, 128), BF16), shape((16, 128), BF16)),
        [pltpu.VMEM((128, 128), F32)],
    )(inbox, jnp.transpose(target, (2, 0, 1)))
    edges = jnp.concatenate([left, right], axis=0)
    sides = [lax.ppermute(edges, "body", trade) for trade in trades(n_body)]
    tile = jnp.concatenate([prof] + sides, axis=0)
    first, second = [lax.ppermute(tile, "patch", trade) for trade in trades(n_patch)]

    stress, pgrad, grads = call(
        step_kernel,
        46,
        (shape((3, TX, TY), F32), shape((V, TX, TY), F32), shape((128, 8, 128), F32)),
        [
            pltpu.VMEM((128, 128), F32),
            pltpu.VMEM((128, Q), BF16),
            pltpu.VMEM((H, 16, TX * TY), BF16),
            pltpu.VMEM((H, 3 * ROWS * C, TY), BF16),
            pltpu.VMEM((H, KB, TY), BF16),
            pltpu.VMEM((H, TX, C, TY), F32),
            pltpu.VMEM((H, NA, C, TY), F32),
            pltpu.VMEM((NA, H * C, TY), BF16),
            pltpu.VMEM((H, 3 * (NA - 1) * C, TY), BF16),
            pltpu.VMEM((H, C, TX * TY), F32),
            pltpu.VMEM((TX, H * C, TY), BF16),
            pltpu.VMEM((8, NA * TY), BF16),
            pltpu.VMEM((C, KB), F32),
        ],
    )(tile, first, second, wa, wat, wf, wb, wh, wht, sel)
    scale = 1.0 / jnp.sqrt(jnp.float32(TX * TY * n_dev))
    total = (jnp.sum(exchange(grads), axis=0) * scale).astype(BF16)
    sums = exchange(jnp.broadcast_to(total[None], (n_dev, 8, 128)))
    grad_a, grad_b, grad_h = call(
        spread_kernel,
        6,
        (shape((F, 3, C), F32), shape((9, C, C), F32), shape((3, H * C), F32)),
    )(sums)
    return (
        jnp.transpose(stress, (1, 2, 0)),
        pgrad,
        jnp.transpose(grad_a, (1, 0, 2)),
        grad_b,
        jnp.transpose(grad_h),
    )


def solution(mesh):
    placed = (
        P(None, ("patch", "body")),
        P(("patch", "body"), None),
        P(("patch", "body")),
        P("patch", "body", None),
        P(),
        P(),
        P(),
    )
    return jax.shard_map(
        shards,
        mesh=mesh,
        in_specs=placed,
        out_specs=(P("patch", "body", None), P(None, "patch", "body"), P(), P(), P()),
        check_vma=False,
    )
```

time: 143 us -> 113 us (0.79)
  Pallas kernels: 55.2 us -> 30.9 us
  starting transfers between devices: 19 us -> 15.3 us
  local copies, waits for them, and re-layouts: 8.37 us -> 5.48 us
    pallas_call x4, Pallas kernels: 55.2 us -> 30.9 us  [run(): pl.pallas_call(kernel, out_shape=out_shape, in_specs=[pl.BlockSpec(memory...]
    ppermute x4, starting transfers between devices: 7.53 us -> 3.81 us  [the longest x2 3.15 us: shards(): sides = [lax.ppermute(edges, 'body', trade) for trade in trades(n_body)]]
    ppermute x4, waiting for transfers between devices: 3.19 us -> 5.42 us  [the longest x2 3.1 us: shards(): sides = [lax.ppermute(edges, 'body', trade) for trade in trades(n_body)]]
    mul x3 -> x1, local copies, waits for them, and re-layouts: 1.79 us -> 0.19 us  [shards(): wb = jnp.transpose(weight_b[::-1], (1, 0, 2)).reshape(C, KB) * half]
    unnamed x16 -> x17, local copies, waits for them, and re-layouts: 2.76 us -> 3.28 us
  transfers between devices with their start and end apart: 5 -> 5, of which waited for: 2 -> 3; matrix products, arithmetic and copies ran while one was open for 6% -> 3% of each run, Pallas kernels for 0% -> 0%
where the time goes in v2:
time: 113 us; the launch traced here: 112 us
  blocking collectives  37.9 us (34%)
  Pallas kernels  30.9 us (27%)
  waiting for transfers between devices  20.6 us (18%)
  starting transfers between devices  15.3 us (14%)
  local copies, waits for them, and re-layouts  5.48 us (5%)
    all_to_all x2, blocking collectives, exchange(): return lax.all_to_all(blocks, AXES, split_axis=0, concat_axis=0, tiled=True)  37.9 us
    pallas_call x4, Pallas kernels, run(): pl.pallas_call(kernel, out_shape=out_shape, in_specs=[pl.BlockSpec(memory...  30.9 us
    all_to_all x1, waiting for transfers between devices, exchange(): return lax.all_to_all(blocks, AXES, split_axis=0, concat_axis=0, tiled=True)  15.2 us
    all_to_all x1, starting transfers between devices, exchange(): return lax.all_to_all(blocks, AXES, split_axis=0, concat_axis=0, tiled=True)  11.5 us
    unnamed x17, local copies, waits for them, and re-layouts  3.28 us
    ppermute x2, starting transfers between devices, shards(): sides = [lax.ppermute(edges, 'body', trade) for trade in trades(n_body)]  3.15 us
    ppermute x2, waiting for transfers between devices, shards(): sides = [lax.ppermute(edges, 'body', trade) for trade in trades(n_body)]  3.1 us
    ppermute x2, waiting for transfers between devices, shards(): lax.ppermute(tile, 'patch', trade)  2.32 us
  transfers between devices with their start and end apart: 5, of which 3 were waited for; matrix products, arithmetic and copies ran while one was open for 3% of the time, Pallas kernels for 0%

profile of v2, /device:TPU:1, one launch (start us, length us, event | category | flops | bytes accessed | tf_op | source)
XLA Modules:
  0.0 112.4 jit_solution(16235685271728725929)
XLA Ops:
  0.6 0.0 copy-start
  0.6 0.0 copy-start.1
  0.7 1.0 copy-done.1
  1.7 0.0 copy-start.2
  1.7 0.7 copy-done.2
  2.4 0.0 copy-start.3
  2.4 0.7 copy-done.3
  3.1 6.4 %shard_map.110 = bf16[4096,128]{1,0:T(8,128)(2,1)} custom-call(bf16[120,2048]{1,0:T(8,128)(2,1)S(1)} %copy-done.1, s32[1,2048]{1,0:T(1,128)S(1)} %bitcast.40, s32[1,2048]{1,0:T(1,128)S(1)} %bitcast.41), custom_call_target="tpu_custom_call" | custom-call | tf_op jit(solution)/shard_map/pallas_call | solution.py:310
  9.5 11.5 %all-to-all-start = ((bf16[128,32,128]{2,1,0:T(8,128)(2,1)}), bf16[128,32,128]{2,1,0:T(8,128)(2,1)S(1)}, u32[]{:S(2)}, u32[]{:S(2)}) async-start(bf16[128,32,128]{2,1,0:T(8,128)(2,1)} %bitcast.2), calls=%async_computation | async-start | bytes 2097152 | tf_op jit(solution)/shard_map/all_to_all | solution.py:327
  21.0 0.0 copy-done
  21.1 0.7 convolution_bitcast_fusion
  21.8 0.1 copy.17
  21.9 0.6 reshape.210
  22.4 0.0 copy-start.6
  22.5 0.0 copy-start.5
  22.5 0.1 pad_bitcast_fusion
  22.6 0.6 copy-done.6
  23.2 0.2 copy-done.5
  23.4 0.1 multiply_bitcast_fusion
  23.5 0.0 copy-start.4
  23.5 0.3 copy.18
  23.8 0.2 copy.19
  24.0 0.3 copy.20
  24.3 0.1 add.110
  24.4 0.1 add.104
  24.5 0.1 add.106
  24.6 0.1 and.56
  24.7 0.3 fusion.3.sel
  25.0 15.2 %all-to-all-done = bf16[128,32,128]{2,1,0:T(8,128)(2,1)S(1)} async-done(((bf16[128,32,128]{2,1,0:T(8,128)(2,1)}), bf16[128,32,128]{2,1,0:T(8,128)(2,1)S(1)}, u32[]{:S(2)}, u32[]{:S(2)}) %all-to-all-start) | async-done | bytes 1048608 | tf_op jit(solution)/shard_map/all_to_all | solution.py:327
  40.3 0.0 copy-done.4
  40.3 1.2 %shard_map.111 = (bf16[256,128]{1,0:T(8,128)(2,1)S(1)}, bf16[16,128]{1,0:T(8,128)(2,1)S(1)}, bf16[16,128]{1,0:T(8,128)(2,1)S(1)}) custom-call(bf16[4096,128]{1,0:T(8,128)(2,1)S(1)} %bitcast.37, f32[3,2,128]{2,1,0:T(2,128)S(1)} %bitcast.42), custom_call_target="tpu_custom_call" | custom-call | tf_op jit(solution)/shard_map/pallas_call | solution.py:310
  41.5 1.0 collective-permute-start
  42.5 2.1 %collective-permute-start.1 = (bf16[32,128]{1,0:T(8,128)(2,1)S(1)}, bf16[32,128]{1,0:T(8,128)(2,1)S(1)}, u32[]{:S(2)}, u32[]{:S(2)}) collective-permute-start(bf16[32,128]{1,0:T(8,128)(2,1)S(1)} %constant_dynamic-update-slice_fusion), channel_id=1, source_target_pairs={{1,2},{2,1},{3,4},{4,3},{5,6},{6,5},{0,0},{7,7},{9,10},{10,9},{11,... | collective-permute-start | bytes 24584 | tf_op jit(solution)/shard_map/ppermute | solution.py:384
  44.6 0.0 collective-permute-done
  44.7 3.1 %collective-permute-done.1 = bf16[32,128]{1,0:T(8,128)(2,1)S(1)} collective-permute-done((bf16[32,128]{1,0:T(8,128)(2,1)S(1)}, bf16[32,128]{1,0:T(8,128)(2,1)S(1)}, u32[]{:S(2)}, u32[]{:S(2)}) %collective-permute-start.1) | collective-permute-done | bytes 8224 | tf_op jit(solution)/shard_map/ppermute | solution.py:384
  47.8 0.0 collective-permute-start.2
  47.8 0.7 collective-permute-start.3
  48.4 0.2 copy.21.wf
  48.6 0.2 copy.22.wb
  48.8 2.3 %collective-permute-done.2.first = bf16[320,128]{1,0:T(8,128)(2,1)S(1)} collective-permute-done((bf16[320,128]{1,0:T(8,128)(2,1)S(1)}, bf16[320,128]{1,0:T(8,128)(2,1)S(1)}, u32[]{:S(2)}, u32[]{:S(2)}) %collective-permute-start.2) | collective-permute-done | bytes 81952 | tf_op jit(solution)/shard_map/ppermute | solution.py:386
  51.1 0.0 collective-permute-done.3.second
  51.1 22.5 %shard_map.112 = (f32[3,2,128]{2,1,0:T(2,128)}, f32[120,2,128]{2,1,0:T(2,128)}, f32[128,8,128]{2,1,0:T(8,128)S(1)}) custom-call(bf16[320,128]{1,0:T(8,128)(2,1)S(1)} %constant_dynamic-update-slice_fusion.2.own, bf16[320,128]{1,0:T(8,128)(2,1)S(1)} %collective-permute-done.2.first, bf16[320,128]{1,0:T(8,128)(2,1)S(1)} %collective-permute-done.3.second, ...), custom_call_target="tpu_custom_call" | custom-call | tf_op jit(solution)/shard_map/pallas_call | solution.py:310
  73.5 22.3 %all_to_all.15 = f32[128,8,128]{2,1,0:T(8,128)S(1)} all-to-all(f32[128,8,128]{2,1,0:T(8,128)S(1)} %get-tuple-element.35), channel_id=1, replica_groups=mesh['patch'=16,'body'=8] {'patch','body'}, dimensions={0} | all-to-all | bytes 1048576 | tf_op jit(solution)/shard_map/all_to_all | solution.py:327
  95.8 0.1 reduce_sum.9
  96.0 15.6 %all_to_all.16.sums = bf16[128,8,128]{2,1,0:T(8,128)(2,1)S(1)} all-to-all(bf16[128,8,128]{2,1,0:T(8,128)(2,1)S(1)} %broadcast_in_dim.2), channel_id=1, replica_groups=mesh['patch'=16,'body'=8] {'patch','body'}, dimensions={0} | all-to-all | bytes 524288 | tf_op jit(solution)/shard_map/all_to_all | solution.py:327
  111.6 0.8 shard_map.113
  (20 shorter events, 0.2 us)
Async XLA Ops:
  0.6 20.4 %copy-start = (bf16[3,5,96]{2,0,1:T(4,128)(2,1)S(1)}, bf16[3,5,96]{2,0,1:T(4,128)(2,1)}, u32[]{:S(2)}) copy-start(bf16[3,5,96]{2,0,1:T(4,128)(2,1)} %param.11) | copy-start | bytes 8644
  0.6 1.0 copy-start.1
  1.7 0.7 copy-start.2
  2.4 0.7 copy-start.3
  9.5 30.7 %all-to-all-start = ((bf16[128,32,128]{2,1,0:T(8,128)(2,1)}), bf16[128,32,128]{2,1,0:T(8,128)(2,1)S(1)}, u32[]{:S(2)}, u32[]{:S(2)}) async-start(bf16[128,32,128]{2,1,0:T(8,128)(2,1)} %bitcast.2), calls=%async_computation | async-start | bytes 2097152 | tf_op jit(solution)/shard_map/all_to_all | solution.py:327
  22.4 0.7 copy-start.6
  22.5 0.9 copy-start.5
  23.5 16.8 %copy-start.4 = (f32[2,128,3]{1,0,2:T(2,128)S(1)}, f32[2,128,3]{1,0,2:T(2,128)}, u32[]{:S(2)}) copy-start(f32[2,128,3]{1,0,2:T(2,128)} %param.10) | copy-start | bytes 9220
  41.5 3.2 %collective-permute-start = (bf16[32,128]{1,0:T(8,128)(2,1)S(1)}, bf16[32,128]{1,0:T(8,128)(2,1)S(1)}, u32[]{:S(2)}, u32[]{:S(2)}) collective-permute-start(bf16[32,128]{1,0:T(8,128)(2,1)S(1)} %constant_dynamic-update-slice_fusion), channel_id=1, source_target_pairs={{0,1},{1,0},{2,3},{3,2},{4,5},{5,4},{6,7},{7,6},{8,9},{9,8},{10,11... | collective-permute-start | bytes 24584 | tf_op jit(solution)/shard_map/ppermute | solution.py:384
  42.5 5.3 %collective-permute-start.1 = (bf16[32,128]{1,0:T(8,128)(2,1)S(1)}, bf16[32,128]{1,0:T(8,128)(2,1)S(1)}, u32[]{:S(2)}, u32[]{:S(2)}) collective-permute-start(bf16[32,128]{1,0:T(8,128)(2,1)S(1)} %constant_dynamic-update-slice_fusion), channel_id=1, source_target_pairs={{1,2},{2,1},{3,4},{4,3},{5,6},{6,5},{0,0},{7,7},{9,10},{10,9},{11,... | collective-permute-start | bytes 24584 | tf_op jit(solution)/shard_map/ppermute | solution.py:384
  47.8 3.3 %collective-permute-start.2 = (bf16[320,128]{1,0:T(8,128)(2,1)S(1)}, bf16[320,128]{1,0:T(8,128)(2,1)S(1)}, u32[]{:S(2)}, u32[]{:S(2)}) collective-permute-start(bf16[320,128]{1,0:T(8,128)(2,1)S(1)} %constant_dynamic-update-slice_fusion.2.own), channel_id=1, source_target_pairs={{0,8},{8,0},{16,24},{24,16},{32,40},{40,32},{48,56},{56,48},{64,72... | collective-permute-start | bytes 245768 | tf_op jit(solution)/shard_map/ppermute | solution.py:386
  47.8 3.3 %collective-permute-start.3 = (bf16[320,128]{1,0:T(8,128)(2,1)S(1)}, bf16[320,128]{1,0:T(8,128)(2,1)S(1)}, u32[]{:S(2)}, u32[]{:S(2)}) collective-permute-start(bf16[320,128]{1,0:T(8,128)(2,1)S(1)} %constant_dynamic-update-slice_fusion.2.own), channel_id=1, source_target_pairs={{8,16},{16,8},{24,32},{32,24},{40,48},{48,40},{56,64},{64,56},{72,... | collective-permute-start | bytes 245768 | tf_op jit(solution)/shard_map/ppermute | solution.py:386
